TPU v7x, 512 devices: a whole 4x8x8 slice. The times are simulated.
512 devices in a mesh: view: 8 (over y_lo, core), tm: 64 (over y_hi, z, x).
Axes of the slice: x: 4, y: 8 (y_hi: 2, y_lo: 4; y = y_hi * 4 + y_lo), z: 8, core: 2. Of those that a mesh axis runs over, the one named last changes fastest.
Arguments:
- frames_x: bfloat16 [8, 64, 384, 1152], P('view', 'tm'), may hold values from -6 to 6
- box_embed: bfloat16 [8, 64, 16, 1152], P('view', 'tm'), may hold values from -6 to 6
- box_count: int32 [8, 64], P('view', 'tm'), may hold values from 1 to 16
- frame_valid: int32 [8, 64], P('view', 'tm'), may hold values 0 or 1
- cycle_link: int32 [8, 2], P('view'), may hold values 0 or 1
- w_qkv: bfloat16 [1152, 3456], P('tm'), may hold values from -0.47140452 to 0.47140452
- w_out: bfloat16 [1152, 1152], P('tm'), may hold values from -0.1875 to 0.1875
- box_gate: float32 [288], replicated, may hold values from -2 to 2
Outputs:
- mixed: bfloat16 [8, 64, 384, 1152], P('view', 'tm')
All inputs are finite; a program needn't handle non-finite values. No bound on the sum of `frame_valid` or of `cycle_link` on one device may be relied on, other than what follows from the above.
Results may differ from a plain program's by a relative error of at most 0.0045.
The roundings to bfloat16 on the way count: a program that leaves them out, or rounds other values in their place, can miss the bound.
Values may be sent and summed in bfloat16 or wider, within the bound.
A program may use at most 128 MiB of HBM per device.

v0:
```python
import jax
import jax.numpy as jnp
from jax import lax
from jax.experimental import pallas as pl
from jax.experimental.pallas import tpu as pltpu
from jax.sharding import PartitionSpec as P

MESH = pl.DeviceIdType.MESH
XC = 640
ZQ = 896
ZW = 2048
QX = 4 * XC
D = 1152
TOKENS = 384
HD = 72
CROSS_HEADS = 8
TIME_HEADS = 4
BOX_HEADS = 4
NEG = -1e30
EXP_SCALE = HD**-0.5 * 1.4426950408889634


def gather_kernel(wq, wo, xin, wx, wz, xn, m, stage, ssem, msem, rxs, rzs, nsem, lsem):
    v = lax.axis_index("view")
    t = lax.axis_index("tm")
    core = lax.rem(v, 2)
    x = lax.rem(t, 4)
    z = lax.rem(t // 4, 8)
    yh = t // 32
    up, down = lax.rem(v + 1, 8), lax.rem(v + 7, 8)
    partner = v + 1 - 2 * core
    d = 1 - 2 * core

    def tm(yy, zz, xx):
        return (yy * 8 + zz) * 4 + xx

    def zat(k):
        return lax.rem(z + d * k + 16, 8)

    barrier = pltpu.get_barrier_semaphore()
    peers = [(up, t), (down, t)]
    peers += [(v, tm(yh, z, lax.rem(x + j, 4))) for j in range(1, 4)]
    peers += [(v, tm(1 - yh, z, lax.rem(x + j, 4))) for j in range(4)]
    peers += [(v, tm(yh, zat(1), x)), (v, tm(yh, zat(-1), x))]
    for p in peers:
        pl.semaphore_signal(barrier, inc=1, device_id=p, device_id_type=MESH)
    pl.semaphore_wait(barrier, len(peers))

    sends = []

    def send(src, dst, rsem, to):
        c = pltpu.make_async_remote_copy(
            src_ref=src,
            dst_ref=dst,
            send_sem=ssem.at[len(sends)],
            recv_sem=rsem,
            device_id=to,
            device_id_type=MESH,
        )
        c.start()
        sends.append(c)

    def arrived(ref, sem):
        pltpu.make_async_copy(ref, ref, sem).wait()

    @pl.when(core == yh)
    def _():
        def pieces(xx):
            cols = pl.ds(pl.multiple_of(xx * XC, 128), XC)
            return [
                (wq.at[:, cols], m.at[x, :, pl.ds(0, XC)], 0),
                (wq.at[:, pl.ds(QX, ZQ)], m.at[x, :, pl.ds(XC, ZQ)], 1),
                (wo, m.at[x, :, pl.ds(XC + ZQ, ZW - ZQ)], 2),
            ]

        out, own = [], []
        for yy, js in ((0, range(4)), (1, range(4))):
            for j in js:
                xx = lax.rem(x + j, 4)
                far = lax.rem(yh + yy, 2)
                for src, dst, k in pieces(xx):
                    if yy == 0 and j == 0:
                        c = pltpu.make_async_copy(src, dst, msem.at[x, k])
                        c.start()
                    else:
                        c = pltpu.make_async_remote_copy(
                            src_ref=src,
                            dst_ref=dst,
                            send_sem=lsem.at[len(out)],
                            recv_sem=msem.at[x, k],
                            device_id=(v, tm(far, z, xx)),
                            device_id_type=MESH,
                        )
                        c.start()
                        out.append(c)
        for c in out:
            c.wait_send()

    send(xin, xn.at[0], nsem.at[0], (up, t))
    send(xin, xn.at[1], nsem.at[1], (down, t))

    row = lax.broadcasted_iota(jnp.int32, (72, 18), 0)
    col = lax.broadcasted_iota(jnp.int32, (72, 18), 1)
    for xx in range(4):
        arrived(m.at[xx, :, pl.ds(0, XC)], msem.at[xx, 0])
        arrived(m.at[xx, :, pl.ds(XC, ZQ)], msem.at[xx, 1])
        arrived(m.at[xx, :, pl.ds(XC + ZQ, ZW - ZQ)], msem.at[xx, 2])
    acc = jnp.zeros((72, XC + ZW), jnp.float32)
    for xx in range(4):
        pick = (row == col + 18 * xx).astype(jnp.bfloat16)
        acc += jnp.dot(pick, m[xx], preferred_element_type=jnp.float32)
    stage[...] = acc.astype(jnp.bfloat16)

    mine = core * 8
    b0 = mine + z
    own = [
        pltpu.make_async_copy(stage.at[:, pl.ds(0, XC)], wx.at[x, b0], rxs.at[x, b0]),
        pltpu.make_async_copy(stage.at[:, pl.ds(XC, ZW)], wz.at[b0], rzs.at[b0]),
    ]
    for c in own:
        c.start()

    def spread(b, srcx, srcz, nxt):
        for n in nxt:
            send(srcx, wx.at[x, b], rxs.at[x, b], (v, tm(yh, n, x)))
            send(srcz, wz.at[b], rzs.at[b], (v, tm(yh, n, x)))
        for j in (1, 3, 2):
            send(srcx, wx.at[x, b], rxs.at[x, b], (v, tm(yh, z, lax.rem(x + j, 4))))
        send(srcx, wx.at[x, b], rxs.at[x, b], (partner, t))
        send(srcz, wz.at[b], rzs.at[b], (partner, t))

    def relay(b):
        for j in (1, 3, 2):
            xx = lax.rem(x + j, 4)
            arrived(wx.at[xx, b], rxs.at[xx, b])
            send(wx.at[xx, b], wx.at[xx, b], rxs.at[xx, b], (partner, t))

    spread(b0, stage.at[:, pl.ds(0, XC)], stage.at[:, pl.ds(XC, ZW)], (zat(1), zat(-1)))
    todo = [b0]
    for s in range(1, 5):
        for sign in (1, -1):
            if sign < 0 and s == 4:
                continue
            b = mine + zat(-s * sign)
            arrived(wx.at[x, b], rxs.at[x, b])
            arrived(wz.at[b], rzs.at[b])
            last = s == 4 or (sign < 0 and s == 3)
            spread(b, wx.at[x, b], wz.at[b], () if last else (zat(sign),))
            todo.append(b)
        if s > 1:
            relay(todo.pop(0))
    for b in todo:
        relay(b)
    for c in own:
        c.wait()
    other = 8 - mine
    for k in range(8):
        b = other + k
        arrived(wz.at[b], rzs.at[b])
        for xx in range(4):
            arrived(wx.at[xx, b], rxs.at[xx, b])
    arrived(xn.at[0], nsem.at[0])
    arrived(xn.at[1], nsem.at[1])
    for c in sends:
        c.wait_send()


def gather(w_qkv, w_out, rows):
    hbm = pl.BlockSpec(memory_space=pl.ANY)
    bf = jnp.bfloat16
    return pl.pallas_call(
        gather_kernel,
        out_shape=(
            jax.ShapeDtypeStruct((4, 16, 72, XC), bf),
            jax.ShapeDtypeStruct((16, 72, ZW), bf),
            jax.ShapeDtypeStruct((2,) + rows.shape, bf),
        ),
        in_specs=[hbm] * 3,
        out_specs=(hbm,) * 3,
        scratch_shapes=[
            pltpu.VMEM((4, 18, XC + ZW), bf),
            pltpu.VMEM((72, XC + ZW), bf),
            pltpu.SemaphoreType.DMA((90,)),
            pltpu.SemaphoreType.DMA((4, 3)),
            pltpu.SemaphoreType.DMA((4, 16)),
            pltpu.SemaphoreType.DMA((16,)),
            pltpu.SemaphoreType.DMA((2,)),
            pltpu.SemaphoreType.DMA((21,)),
        ],
        compiler_params=pltpu.CompilerParams(collective_id=0, has_side_effects=True),
        name="gather",
    )(w_qkv, w_out, rows)


def attend_kernel(
    x_ref, xn_ref, wx_ref, wz_ref, box_ref, cnt_ref, val_ref, link_ref, gate_ref, out_ref,
    qkv, nbr, tsend, tqkv, tout, timed, kvb, bkv, qc, kc, vc, qb, kb, vb, oh,
    ts_send, ts_recv, to_send, to_recv, ba_send, ba_recv, br_send, br_recv, own_sem,
):
    bf, f32 = jnp.bfloat16, jnp.float32
    v = lax.axis_index("view")
    t = lax.axis_index("tm")
    core = lax.rem(v, 2)
    x = lax.rem(t, 4)
    z = lax.rem(t // 4, 8)
    yh = t // 32
    d = 1 - 2 * core
    v4 = lax.rem(v + 4, 8)
    owner = (t // 4) * 3 + x
    base = (t * 3) // 4

    def tm(yy, zz, xx):
        return (yy * 8 + zz) * 4 + xx

    def zat(k):
        return lax.rem(z + d * k + 16, 8)

    plane = [tm(yh, z, lax.rem(x + j, 4)) for j in range(1, 4)]
    plane += [tm(1 - yh, z, lax.rem(x + j, 4)) for j in range(4)]
    barrier = pltpu.get_barrier_semaphore()

    @pl.loop(0, 64)
    def _(i):
        pl.semaphore_signal(barrier, inc=1, device_id=(v4, i), device_id_type=MESH)

    for p in plane + [tm(yh, zat(1), x), tm(yh, zat(-1), x)]:
        pl.semaphore_signal(barrier, inc=1, device_id=(v, p), device_id_type=MESH)

    def mm(a, b):
        return jnp.dot(a, b, preferred_element_type=f32)

    rows = x_ref[...]
    for i in range(4):
        qkv[:, i * XC : (i + 1) * XC] = mm(rows, wx_ref[i])
    qkv[:, QX : QX + ZQ] = mm(rows, wz_ref[:, :ZQ])

    tq = [qkv[:, c * 128 : c * 128 + 896] for c in (4, 13)]
    tq.append(jnp.concatenate([qkv[:, 2816:3456], qkv[:, 0:256]], axis=1))
    lane = lax.broadcasted_iota(jnp.int32, (TOKENS, 896), 1)
    packed = pltpu.roll(tq[0], 896 - 64, 1)
    packed = jnp.where(lane < 288, packed, pltpu.roll(tq[1], 288 - 64, 1))
    packed = jnp.where(lane < 576, packed, pltpu.roll(tq[2], 576 - 64, 1))
    tsend[...] = packed.astype(bf).reshape(48, 8, 896)

    boxes = box_ref[...]
    bv = jnp.concatenate([mm(boxes, wx_ref[3][:, 0:384]), mm(boxes, wz_ref[:, 512:896])], axis=1)
    slot = lax.broadcasted_iota(jnp.int32, (16, 768), 0)
    blane = lax.broadcasted_iota(jnp.int32, (16, 768), 1)
    live = jnp.logical_and(slot < cnt_ref[0, 0], val_ref[0, 0] == 1)
    bv = jnp.where(blane == 0, jnp.where(live, 0.0, NEG), bv)
    kvb[...] = bv.astype(bf)

    pl.semaphore_wait(barrier, 73)

    def time_copy(i):
        o = lax.rem(i + base, 48)
        return pltpu.make_async_remote_copy(
            src_ref=tsend.at[o],
            dst_ref=tqkv.at[t],
            send_sem=ts_send.at[i],
            recv_sem=ts_recv.at[t],
            device_id=(v4, (o // 3) * 4 + lax.rem(o, 3)),
            device_id_type=MESH,
        )

    @pl.loop(0, 48)
    def _(i):
        time_copy(i).start()

    own = pltpu.make_async_copy(kvb, bkv.at[t], own_sem)
    own.start()
    first = []
    for k, p in enumerate(plane):
        c = pltpu.make_async_remote_copy(
            src_ref=kvb,
            dst_ref=bkv.at[t],
            send_sem=ba_send.at[k],
            recv_sem=ba_recv.at[yh * 4 + x],
            device_id=(v, p),
            device_id_type=MESH,
        )
        c.start()
        first.append(c)

    near = xn_ref[...].reshape(2 * TOKENS, D)
    nbr[:, 0:128] = mm(near, wx_ref[1][:, 512:640])
    nbr[:, 128:640] = mm(near, wx_ref[2][:, 0:512])
    nbr[:, 640:896] = mm(near, wx_ref[3][:, 384:640])
    nbr[:, 896:1280] = mm(near, wz_ref[:, 0:384])

    def tile(a, off, fill):
        piece = pltpu.roll(a, (a.shape[1] - off) % a.shape[1], 1)[:, :128] if off else a[:, :128]
        at = lax.broadcasted_iota(jnp.int32, piece.shape, 1)
        return jnp.where(at < HD, piece, jnp.where(at == HD, fill, 0.0)).astype(bf)

    def head(ref, r0, r1, c, fill):
        lo = c // 128 * 128
        a = ref[r0:r1, lo : min(lo + 256, ref.shape[1])]
        return tile(a, c - lo, fill)

    gone = [jnp.where(link_ref[0, i] > 0, 0.0, NEG) for i in range(2)]
    n = TOKENS
    for h in range(CROSS_HEADS):
        qc[h] = head(qkv, 0, n, HD * h, 1.0)
        for s, (ref, r0, ck, cv, fill) in enumerate(
            (
                (nbr, 0, 0, 640, gone[0]),
                (qkv, 0, D, 2 * D, 0.0),
                (nbr, n, 0, 640, gone[1]),
            )
        ):
            kc[h, s * n : (s + 1) * n] = head(ref, r0, r0 + n, ck + HD * h, fill)
            vc[h, s * n : (s + 1) * n] = head(ref, r0, r0 + n, cv + HD * h, 1.0)
    at0 = (CROSS_HEADS + TIME_HEADS) * HD
    for h in range(BOX_HEADS):
        qb[h] = head(qkv, 0, n, at0 + HD * h, 1.0)
        kb[h, 0:n] = head(qkv, 0, n, D + at0 + HD * h, 0.0)
        vb[h, 0:n] = head(qkv, 0, n, 2 * D + at0 + HD * h, 1.0)

    own.wait()
    for yy in range(2):
        for j in range(4):
            xx = lax.rem(x + j, 4)

            def take(yy=yy, xx=xx):
                ref = bkv.at[tm(lax.rem(yh + yy, 2), z, xx)]
                pltpu.make_async_copy(ref, ref, ba_recv.at[lax.rem(yh + yy, 2) * 4 + xx]).wait()

            if yy or j:
                take()

    def group(yy, zz):
        return bkv.at[pl.ds(tm(yy, zz, 0), 4)]

    def ring(yy, zz, to, k):
        return pltpu.make_async_remote_copy(
            src_ref=group(yy, zz),
            dst_ref=group(yy, zz),
            send_sem=br_send.at[k],
            recv_sem=br_recv.at[yy * 8 + zz],
            device_id=(v, tm(yh, to, x)),
            device_id_type=MESH,
        )

    sent = []

    def start(c):
        c.start()
        sent.append(c)

    for yy in range(2):
        for sign in (1, -1):
            start(ring(yy, z, zat(sign), len(sent)))

    def relay(s):
        for sign in (1, -1):
            if sign < 0 and s == 4:
                continue
            zz = zat(-s * sign)
            for yy in range(2):
                ref = group(yy, zz)
                pltpu.make_async_copy(ref, ref, br_recv.at[yy * 8 + zz]).wait()
                if s < (4 if sign > 0 else 3):
                    start(ring(yy, zz, zat(sign), len(sent)))

    def softmax_dot(q, k, val):
        s = lax.dot_general(q, k, (((1,), (1,)), ((), ())), preferred_element_type=f32)
        top = jnp.max(s, axis=1, keepdims=True)
        p = jnp.exp2((s - top) * EXP_SCALE).astype(bf)
        return mm(p, val)

    def heads(first_head, count, q_ref, k_ref, v_ref, out0):
        @pl.loop(first_head, first_head + count)
        def _(h):
            for r in range(0, n, 128):
                o = softmax_dot(q_ref[h, r : r + 128], k_ref[h], v_ref[h])
                oh[out0 + h, r : r + 128] = o * (1.0 / o[:, HD : HD + 1])

    for s in range(1, 5):
        heads(2 * (s - 1), 2, qc, kc, vc, 0)
        relay(s)

    @pl.loop(0, 64)
    def _(i):
        ref = tqkv.at[i]

        @pl.when(x < 3)
        def _():
            pltpu.make_async_copy(ref, ref, ts_recv.at[i]).wait()

    def back(i):
        f = lax.rem(i + t, 64)
        return pltpu.make_async_remote_copy(
            src_ref=tout.at[f],
            dst_ref=timed.at[owner],
            send_sem=to_send.at[i],
            recv_sem=to_recv.at[owner],
            device_id=(v4, f),
            device_id_type=MESH,
        )

    @pl.when(x < 3)
    def _():
        a = tqkv[...].reshape(512, 896).astype(f32)
        r = lax.broadcasted_iota(jnp.int32, (512, 512), 0)
        c = lax.broadcasted_iota(jnp.int32, (512, 512), 1)
        other = jnp.where(jnp.bitwise_and(r, 7) == jnp.bitwise_and(c, 7), 0.0, NEG)
        outs = []
        for h in range(TIME_HEADS):
            q = tile(a, HD * h, 0.0)
            k = tile(a, 288 + HD * h, 0.0)
            val = tile(a, 576 + HD * h, 1.0)
            s = lax.dot_general(q, k, (((1,), (1,)), ((), ())), preferred_element_type=f32) + other
            top = jnp.max(s, axis=1, keepdims=True)
            p = jnp.exp2((s - top) * EXP_SCALE).astype(bf)
            o = mm(p, val)
            outs.append(o * (1.0 / o[:, HD : HD + 1]))
        tout[...] = joined(outs).astype(bf).reshape(64, 8, 384)

    for r in range(0, 1024, 256):
        a = bkv[r // 16 : r // 16 + 16].reshape(256, 768).astype(f32)
        fill = a[:, 0:1]
        for h in range(BOX_HEADS):
            kb[h, n + r : n + r + 256] = tile(a, 96 + HD * h, fill)
            vb[h, n + r : n + r + 256] = tile(a, 480 + HD * h, 1.0)

    @pl.when(x < 3)
    def _():
        @pl.loop(0, 64)
        def _(i):
            back(i).start()

    heads(0, BOX_HEADS, qb, kb, vb, CROSS_HEADS)

    total = rows.astype(f32)
    crossed = joined([oh[h] for h in range(CROSS_HEADS)]).astype(bf)
    total += mm(crossed[:, :576], wz_ref[0:576, ZQ:ZW])
    boxed = joined([oh[CROSS_HEADS + h] for h in range(BOX_HEADS)])[:, :288]
    boxed = (boxed * jnp.tanh(gate_ref[...])).astype(bf)
    total += mm(boxed, wz_ref[864:1152, ZQ:ZW])

    @pl.loop(0, 48)
    def _(i):
        ref = timed.at[i]
        pltpu.make_async_copy(ref, ref, to_recv.at[i]).wait()

    both = timed[...].reshape(n, 384)
    total += mm(both[:, :288], wz_ref[576:864, ZQ:ZW])
    out_ref[...] = total.astype(bf)

    @pl.loop(0, 48)
    def _(i):
        time_copy(i).wait_send()

    @pl.when(x < 3)
    def _():
        @pl.loop(0, 64)
        def _(i):
            back(i).wait_send()

    for c in first + sent:
        c.wait_send()


def joined(outs):
    width = -(-len(outs) * HD // 128) * 128
    rows = outs[0].shape[0]
    at = lax.broadcasted_iota(jnp.int32, (rows, 128), 1)
    blank = jnp.zeros((rows, 128), jnp.float32)
    done = []
    for c in range(width // 128):
        piece = blank
        for h, o in enumerate(outs):
            lo = h * HD - c * 128
            if lo >= 128 or lo + HD <= 0:
                continue
            moved = pltpu.roll(o, lo % 128, 1) if lo % 128 else o
            keep = jnp.logical_and(at >= lo, at < lo + HD)
            piece = jnp.where(keep, moved, piece)
        done.append(piece)
    return jnp.concatenate(done, axis=1)


def attend(rows, near, wx, wz, boxes, count, valid, link, gate):
    bf, f32 = jnp.bfloat16, jnp.float32
    vmem = pl.BlockSpec(memory_space=pltpu.VMEM)
    smem = pl.BlockSpec(memory_space=pltpu.SMEM)
    n = TOKENS
    dma = pltpu.SemaphoreType.DMA
    return pl.pallas_call(
        attend_kernel,
        out_shape=jax.ShapeDtypeStruct(rows.shape, bf),
        in_specs=[vmem] * 5 + [smem] * 3 + [vmem],
        out_specs=vmem,
        scratch_shapes=[
            pltpu.VMEM((n, 3 * D), f32),
            pltpu.VMEM((2 * n, 1280), f32),
            pltpu.VMEM((48, 8, 896), bf),
            pltpu.VMEM((64, 8, 896), bf),
            pltpu.VMEM((64, 8, 384), bf),
            pltpu.VMEM((48, 8, 384), bf),
            pltpu.VMEM((16, 768), bf),
            pltpu.VMEM((64, 16, 768), bf),
            pltpu.VMEM((8, n, 128), bf),
            pltpu.VMEM((8, 3 * n, 128), bf),
            pltpu.VMEM((8, 3 * n, 128), bf),
            pltpu.VMEM((4, n, 128), bf),
            pltpu.VMEM((4, n + 1024, 128), bf),
            pltpu.VMEM((4, n + 1024, 128), bf),
            pltpu.VMEM((12, n, 128), f32),
            dma((48,)), dma((64,)), dma((64,)), dma((48,)),
            dma((7,)), dma((8,)), dma((16,)), dma((16,)), dma,
        ],
        compiler_params=pltpu.CompilerParams(
            collective_id=1, has_side_effects=True, vmem_limit_bytes=60 << 20
        ),
        name="attend",
    )(rows, near, wx, wz, boxes, count, valid, link, gate)


def per_device(frames_x, box_embed, box_count, frame_valid, cycle_link, w_qkv, w_out, box_gate):
    rows = frames_x.reshape(TOKENS, D)
    boxes = box_embed.reshape(16, D)
    wx, wz, near = gather(w_qkv, w_out, rows)
    result = attend(
        rows,
        near,
        wx.reshape(4, D, XC),
        wz.reshape(D, ZW),
        boxes,
        box_count,
        frame_valid,
        cycle_link,
        box_gate.reshape(1, BOX_HEADS * HD),
    )
    return result.reshape(frames_x.shape)


def solution(mesh):
    in_specs = (
        P("view", "tm", None, None),
        P("view", "tm", None, None),
        P("view", "tm"),
        P("view", "tm"),
        P("view", None),
        P("tm", None),
        P("tm", None),
        P(),
    )
    out_specs = P("view", "tm", None, None)
    return jax.shard_map(
        per_device, mesh=mesh, in_specs=in_specs, out_specs=out_specs, check_vma=False
    )
```

profile of v0, /device:TPU:12, one launch (start us, length us, event | category | flops | bytes accessed | tf_op | source)
XLA Modules:
  0.0 179.4 jit_solution(2217968026215863954)
XLA Ops:
  1.3 1.2 reshape.22.gate_ref
  2.5 75.5 %gather.1 = (bf16[4,16,72,640]{3,2,1,0:T(8,128)(2,1)}, bf16[16,72,2048]{2,1,0:T(8,128)(2,1)}, bf16[2,384,1152]{2,1,0:T(8,128)(2,1)}) custom-call(bf16[18,3456]{1,0:T(8,128)(2,1)} %wq.1, bf16[18,1152]{1,0:T(8,128)(2,1)} %wo.1, bf16[384,1152]{1,0:T(8,128)(2,1)} %bitcast.8), custom_call_target="tpu_custom_call" | custom-call | tf_op jit(solution)/shard_map/gather/pallas_call | solution.py:171
  78.0 99.2 %attend.1 = bf16[384,1152]{1,0:T(8,128)(2,1)} custom-call(bf16[384,1152]{1,0:T(8,128)(2,1)} %bitcast.9, bf16[2,384,1152]{2,1,0:T(8,128)(2,1)} %get-tuple-element.8.xn_ref, bf16[4,1152,640]{2,1,0:T(8,128)(2,1)} %bitcast.5, bf16[1152,2048]{1,0:T(8,128)(2,1)} %bitcast.6, bf16[16,1152]{1,0:T(8,128)(2,1)} %bitcast.10, s32[1,1]{1,0:T(1,128)S(6)} %copy.10.cnt_ref, ...), custom_call_target="tpu_custom_call" | custom-call | tf_op jit(solution)/shard_map/attend/pallas_call | solution.py:490
  177.3 2.1 %copy.12 = bf16[1,1,384,1152]{3,2,1,0:T(8,128)(2,1)} copy(bf16[1,1,384,1152]{3,2,1,0:T(8,128)(2,1)} %bitcast.7) | data formatting | bytes 1769472
where the time goes:
time: 180 us; the launch traced here: 179 us
  Pallas kernels  175 us (97%)
  local copies, waits for them, and re-layouts  3.39 us (2%)
    pallas_call x1, Pallas kernels, attend(): pl.pallas_call(attend_kernel, out_shape=jax.ShapeDtypeStruct(rows.shape,...  99.2 us
    pallas_call x1, Pallas kernels, gather(): pl.pallas_call(gather_kernel, out_shape=(jax.ShapeDtypeStruct((4, 16, 72,...  75.5 us

commit v1 on v0

v1 whole, which is shorter than its diff:
```python
import jax
import jax.numpy as jnp
from jax import lax
from jax.experimental import pallas as pl
from jax.experimental.pallas import tpu as pltpu
from jax.sharding import PartitionSpec as P

MESH = pl.DeviceIdType.MESH
XC = 768
ZQ = 384
ZW = 1536
QX = 4 * XC
D = 1152
TOKENS = 384
HD = 72
CROSS_HEADS = 8
TIME_HEADS = 4
BOX_HEADS = 4
NEG = -1e30
EXP_SCALE = HD**-0.5 * 1.4426950408889634


def layer_kernel(
    wq, wo, x_ref, box_ref, cnt_ref, val_ref, link_ref, gate_ref, out_ref,
    wx, wz, xn, m, stage,
    qkv, nbr, tsend, tqkv, tout, timed, kvb, bkv, qc, kc, vc, qb, kb, vb, oh,
    ssem, msem, rxs, rzs, nsem, lsem,
    ts_send, ts_recv, to_send, to_recv, ba_send, ba_recv, br_send, br_recv, own_sem,
):
    bf, f32 = jnp.bfloat16, jnp.float32
    n = TOKENS
    v = lax.axis_index("view")
    t = lax.axis_index("tm")
    core = lax.rem(v, 2)
    x = lax.rem(t, 4)
    z = lax.rem(t // 4, 8)
    yh = t // 32
    d = 1 - 2 * core
    up, down = lax.rem(v + 1, 8), lax.rem(v + 7, 8)
    partner = v + 1 - 2 * core
    v4 = lax.rem(v + 4, 8)
    owner = (t // 4) * 3 + x
    base = (t * 3) // 4
    right, left, across = [lax.rem(x + j, 4) for j in (1, 3, 2)]

    def tm(yy, zz, xx):
        return (yy * 8 + zz) * 4 + xx

    def zat(k):
        return lax.rem(z + d * k + 16, 8)

    plane = [tm(yh, z, lax.rem(x + j, 4)) for j in range(1, 4)]
    plane += [tm(1 - yh, z, lax.rem(x + j, 4)) for j in range(4)]
    barrier = pltpu.get_barrier_semaphore()

    @pl.loop(0, 64)
    def _(i):
        pl.semaphore_signal(barrier, inc=1, device_id=(v4, i), device_id_type=MESH)

    for p in plane + [tm(yh, zat(1), x), tm(yh, zat(-1), x)]:
        pl.semaphore_signal(barrier, inc=1, device_id=(v, p), device_id_type=MESH)
    for p in (up, down):
        pl.semaphore_signal(barrier, inc=1, device_id=(p, t), device_id_type=MESH)
    pl.semaphore_wait(barrier, 75)

    sends = []

    def send(src, dst, rsem, to):
        c = pltpu.make_async_remote_copy(
            src_ref=src,
            dst_ref=dst,
            send_sem=ssem.at[len(sends)],
            recv_sem=rsem,
            device_id=to,
            device_id_type=MESH,
        )
        c.start()
        sends.append(c)

    def arrived(ref, sem):
        pltpu.make_async_copy(ref, ref, sem).wait()

    @pl.when(core == yh)
    def _():
        out = []
        for half, view in ((yh, v), (1 - yh, v4)):
            for j in (2, 1, 3, 0):
                xx = lax.rem(x + j, 4)
                cols = pl.ds(pl.multiple_of(xx * XC, 128), XC)
                for k, (src, lo, width) in enumerate(
                    (
                        (wq.at[:, cols], 0, XC),
                        (wq.at[:, pl.ds(QX, ZQ)], XC, ZQ),
                        (wo, XC + ZQ, ZW - ZQ),
                    )
                ):
                    dst = m.at[x, :, pl.ds(lo, width)]
                    if view is v and j == 0:
                        pltpu.make_async_copy(src, dst, msem.at[x, k]).start()
                        continue
                    c = pltpu.make_async_remote_copy(
                        src_ref=src,
                        dst_ref=dst,
                        send_sem=lsem.at[len(out)],
                        recv_sem=msem.at[x, k],
                        device_id=(view, tm(half, z, xx)),
                        device_id_type=MESH,
                    )
                    c.start()
                    out.append(c)
        for c in out:
            c.wait_send()

    row = lax.broadcasted_iota(jnp.int32, (72, 18), 0)
    col = lax.broadcasted_iota(jnp.int32, (72, 18), 1)
    for xx in range(4):
        arrived(m.at[xx, :, pl.ds(0, XC)], msem.at[xx, 0])
        arrived(m.at[xx, :, pl.ds(XC, ZQ)], msem.at[xx, 1])
        arrived(m.at[xx, :, pl.ds(XC + ZQ, ZW - ZQ)], msem.at[xx, 2])
    acc = jnp.zeros((72, XC + ZW), f32)
    for xx in range(4):
        pick = (row == col + 18 * xx).astype(bf)
        acc += jnp.dot(pick, m[xx], preferred_element_type=f32)
    stage[...] = acc.astype(bf)

    mine = core * 8
    b0 = mine + z
    fresh = [
        pltpu.make_async_copy(stage.at[:, pl.ds(0, XC)], wx.at[x, b0], rxs.at[x, b0]),
        pltpu.make_async_copy(stage.at[:, pl.ds(XC, ZW)], wz.at[b0], rzs.at[b0]),
    ]
    for c in fresh:
        c.start()

    def forward(xx, b, to):
        send(wx.at[xx, b], wx.at[xx, b], rxs.at[xx, b], to)

    def spread(b, srcx, srcz, nxt):
        for k in nxt:
            send(srcx, wx.at[x, b], rxs.at[x, b], (v, tm(yh, k, x)))
            send(srcz, wz.at[b], rzs.at[b], (v, tm(yh, k, x)))
        for xx in (right, left):
            send(srcx, wx.at[x, b], rxs.at[x, b], (v, tm(yh, z, xx)))
        send(srcx, wx.at[x, b], rxs.at[x, b], (partner, t))
        send(srcz, wz.at[b], rzs.at[b], (partner, t))

    def relay_x(b, sign):
        arrived(wx.at[left, b], rxs.at[left, b])
        if sign > 0:
            forward(left, b, (v, tm(yh, z, right)))
        forward(left, b, (partner, t))
        arrived(wx.at[right, b], rxs.at[right, b])
        if sign < 0:
            forward(right, b, (v, tm(yh, z, left)))
        forward(right, b, (partner, t))

    def last_x(b):
        arrived(wx.at[across, b], rxs.at[across, b])
        forward(across, b, (partner, t))

    spread(b0, stage.at[:, pl.ds(0, XC)], stage.at[:, pl.ds(XC, ZW)], (zat(1), zat(-1)))
    send(x_ref, xn.at[0], nsem.at[0], (up, t))
    send(x_ref, xn.at[1], nsem.at[1], (down, t))
    todo, late = [(b0, -1)], []
    for s in range(1, 5):
        for sign in (1, -1):
            if sign < 0 and s == 4:
                continue
            b = mine + zat(-s * sign)
            arrived(wx.at[x, b], rxs.at[x, b])
            arrived(wz.at[b], rzs.at[b])
            last = s == 4 or (sign < 0 and s == 3)
            spread(b, wx.at[x, b], wz.at[b], () if last else (zat(sign),))
            todo.append((b, sign))
            b, sign = todo.pop(0)
            relay_x(b, sign)
            late.append(b)
            if len(late) > 2:
                last_x(late.pop(0))
    for b, sign in todo:
        relay_x(b, sign)
        late.append(b)
    for b in late:
        last_x(b)
    for c in fresh:
        c.wait()
    other = 8 - mine
    for k in range(8):
        b = other + k
        arrived(wz.at[b], rzs.at[b])
        for xx in range(4):
            arrived(wx.at[xx, b], rxs.at[xx, b])

    def mm(a, b):
        return jnp.dot(a, b, preferred_element_type=f32)

    def chunk(i, lo, hi):
        return wx[i, :, :, lo:hi].reshape(D, hi - lo)

    def tail(lo, hi):
        return wz[:, :, lo:hi].reshape(D, hi - lo)

    boxes = box_ref[...]
    bk = jnp.concatenate([mm(boxes, chunk(2, 384, 768)), mm(boxes, tail(0, 384))], axis=1)
    slot = lax.broadcasted_iota(jnp.int32, (16, 768), 0)
    blane = lax.broadcasted_iota(jnp.int32, (16, 768), 1)
    live = jnp.logical_and(slot < cnt_ref[0, 0], val_ref[0, 0] == 1)
    bv = jnp.where(blane < 288, pltpu.roll(bk, 768 - 96, 1), pltpu.roll(bk, 768 - 192, 1))
    bv = jnp.where(blane == 576, jnp.where(live, 0.0, NEG), bv)
    kvb[...] = bv[:, :640].astype(bf)

    rows = x_ref[...]
    qkv[:, 0:XC] = mm(rows, chunk(0, 0, XC))

    own = pltpu.make_async_copy(kvb, bkv.at[t], own_sem)
    own.start()
    first = []
    for k, p in enumerate(plane):
        c = pltpu.make_async_remote_copy(
            src_ref=kvb,
            dst_ref=bkv.at[t],
            send_sem=ba_send.at[k],
            recv_sem=ba_recv.at[yh * 4 + x],
            device_id=(v, p),
            device_id_type=MESH,
        )
        c.start()
        first.append(c)

    for i in range(1, 4):
        qkv[:, i * XC : (i + 1) * XC] = mm(rows, chunk(i, 0, XC))
    qkv[:, QX : QX + ZQ] = mm(rows, tail(0, ZQ))

    tq = [qkv[:, c * 128 : c * 128 + 896] for c in (4, 13)]
    tq.append(jnp.concatenate([qkv[:, 2816:3456], qkv[:, 0:256]], axis=1))
    lane = lax.broadcasted_iota(jnp.int32, (n, 896), 1)
    packed = pltpu.roll(tq[0], 896 - 64, 1)
    packed = jnp.where(lane < 288, packed, pltpu.roll(tq[1], 288 - 64, 1))
    packed = jnp.where(lane < 576, packed, pltpu.roll(tq[2], 576 - 64, 1))
    tsend[...] = packed.astype(bf).reshape(48, 8, 896)

    def time_copy(i):
        o = lax.rem(i + base, 48)
        return pltpu.make_async_remote_copy(
            src_ref=tsend.at[o],
            dst_ref=tqkv.at[t],
            send_sem=ts_send.at[i],
            recv_sem=ts_recv.at[t],
            device_id=(v4, (o // 3) * 4 + lax.rem(o, 3)),
            device_id_type=MESH,
        )

    def send_time(lo, hi):
        @pl.loop(lo, hi)
        def _(i):
            time_copy(i).start()

    own.wait()
    for yy in range(2):
        for j in range(4):
            if yy or j:
                half, xx = lax.rem(yh + yy, 2), lax.rem(x + j, 4)
                arrived(bkv.at[tm(half, z, xx)], ba_recv.at[half * 4 + xx])

    def group(yy, zz):
        return bkv.at[pl.ds(tm(yy, zz, 0), 4)]

    def ring(yy, zz, to, k):
        return pltpu.make_async_remote_copy(
            src_ref=group(yy, zz),
            dst_ref=group(yy, zz),
            send_sem=br_send.at[k],
            recv_sem=br_recv.at[yy * 8 + zz],
            device_id=(v, tm(yh, to, x)),
            device_id_type=MESH,
        )

    sent = []

    def start(c):
        c.start()
        sent.append(c)

    for yy in range(2):
        for sign in (1, -1):
            start(ring(yy, z, zat(sign), len(sent)))

    def relay(s):
        for sign in (1, -1):
            if sign < 0 and s == 4:
                continue
            zz = zat(-s * sign)
            for yy in range(2):
                arrived(group(yy, zz), br_recv.at[yy * 8 + zz])
                if s < (4 if sign > 0 else 3):
                    start(ring(yy, zz, zat(sign), len(sent)))

    send_time(0, 24)

    arrived(xn.at[0], nsem.at[0])
    arrived(xn.at[1], nsem.at[1])
    near = xn[...].reshape(2 * n, D)
    nbr[:, 0:384] = mm(near, chunk(1, 384, 768))
    nbr[:, 384:640] = mm(near, chunk(2, 0, 256))
    nbr[:, 640:1280] = mm(near, chunk(3, 0, 640))

    def tile(a, off, fill):
        piece = pltpu.roll(a, (a.shape[1] - off) % a.shape[1], 1)[:, :128] if off else a[:, :128]
        at = lax.broadcasted_iota(jnp.int32, piece.shape, 1)
        return jnp.where(at < HD, piece, jnp.where(at == HD, fill, 0.0)).astype(bf)

    def head(ref, r0, r1, c, fill):
        lo = c // 128 * 128
        a = ref[r0:r1, lo : min(lo + 256, ref.shape[1])]
        return tile(a, c - lo, fill)

    gone = [jnp.where(link_ref[0, i] > 0, 0.0, NEG) for i in range(2)]
    for h in range(CROSS_HEADS):
        qc[h] = head(qkv, 0, n, HD * h, 1.0)
        for s, (ref, r0, ck, cv, fill) in enumerate(
            (
                (nbr, 0, 0, 640, gone[0]),
                (qkv, 0, D, 2 * D, 0.0),
                (nbr, n, 0, 640, gone[1]),
            )
        ):
            kc[h, s * n : (s + 1) * n] = head(ref, r0, r0 + n, ck + HD * h, fill)
            vc[h, s * n : (s + 1) * n] = head(ref, r0, r0 + n, cv + HD * h, 1.0)
    at0 = (CROSS_HEADS + TIME_HEADS) * HD
    for h in range(BOX_HEADS):
        qb[h] = head(qkv, 0, n, at0 + HD * h, 1.0)
        kb[h, 0:n] = head(qkv, 0, n, D + at0 + HD * h, 0.0)
        vb[h, 0:n] = head(qkv, 0, n, 2 * D + at0 + HD * h, 1.0)

    def softmax_dot(q, k, val):
        s = lax.dot_general(q, k, (((1,), (1,)), ((), ())), preferred_element_type=f32)
        top = jnp.max(s, axis=1, keepdims=True)
        p = jnp.exp2((s - top) * EXP_SCALE).astype(bf)
        return mm(p, val)

    def heads(first_head, count, q_ref, k_ref, v_ref, out0):
        @pl.loop(first_head, first_head + count)
        def _(h):
            for r in range(0, n, 128):
                o = softmax_dot(q_ref[h, r : r + 128], k_ref[h], v_ref[h])
                oh[out0 + h, r : r + 128] = o * (1.0 / o[:, HD : HD + 1])

    for s in range(1, 5):
        relay(s)
        if s == 1:
            send_time(24, 48)
        heads(2 * (s - 1), 2, qc, kc, vc, 0)

    @pl.loop(0, 64)
    def _(i):
        ref = tqkv.at[i]

        @pl.when(x < 3)
        def _():
            pltpu.make_async_copy(ref, ref, ts_recv.at[i]).wait()

    def back(i):
        f = lax.rem(i + t, 64)
        return pltpu.make_async_remote_copy(
            src_ref=tout.at[f],
            dst_ref=timed.at[owner],
            send_sem=to_send.at[i],
            recv_sem=to_recv.at[owner],
            device_id=(v4, f),
            device_id_type=MESH,
        )

    @pl.when(x < 3)
    def _():
        a = tqkv[...].reshape(512, 896).astype(f32)
        r = lax.broadcasted_iota(jnp.int32, (512, 512), 0)
        c = lax.broadcasted_iota(jnp.int32, (512, 512), 1)
        other = jnp.where(jnp.bitwise_and(r, 7) == jnp.bitwise_and(c, 7), 0.0, NEG)
        outs = []
        for h in range(TIME_HEADS):
            q = tile(a, HD * h, 0.0)
            k = tile(a, 288 + HD * h, 0.0)
            val = tile(a, 576 + HD * h, 1.0)
            s = lax.dot_general(q, k, (((1,), (1,)), ((), ())), preferred_element_type=f32) + other
            top = jnp.max(s, axis=1, keepdims=True)
            p = jnp.exp2((s - top) * EXP_SCALE).astype(bf)
            o = mm(p, val)
            outs.append(o * (1.0 / o[:, HD : HD + 1]))
        tout[...] = joined(outs).astype(bf).reshape(64, 8, 384)

    for r in range(0, 1024, 256):
        a = bkv[r // 16 : r // 16 + 16].reshape(256, 640).astype(f32)
        fill = a[:, 576:577]
        for h in range(BOX_HEADS):
            kb[h, n + r : n + r + 256] = tile(a, HD * h, fill)
            vb[h, n + r : n + r + 256] = tile(a, 288 + HD * h, 1.0)

    @pl.when(x < 3)
    def _():
        @pl.loop(0, 64)
        def _(i):
            back(i).start()

    heads(0, BOX_HEADS, qb, kb, vb, CROSS_HEADS)

    total = rows.astype(f32)
    crossed = joined([oh[h] for h in range(CROSS_HEADS)]).astype(bf)
    total += mm(crossed[:, :576], wz[0:8, :, ZQ:ZW].reshape(576, D))
    boxed = joined([oh[CROSS_HEADS + h] for h in range(BOX_HEADS)])[:, :288]
    boxed = (boxed * jnp.tanh(gate_ref[...].reshape(1, BOX_HEADS * HD))).astype(bf)
    total += mm(boxed, wz[12:16, :, ZQ:ZW].reshape(288, D))

    @pl.loop(0, 48)
    def _(i):
        ref = timed.at[i]
        pltpu.make_async_copy(ref, ref, to_recv.at[i]).wait()

    both = timed[...].reshape(n, 384)
    total += mm(both[:, :288], wz[8:12, :, ZQ:ZW].reshape(288, D))
    out_ref[...] = total.astype(bf)

    @pl.loop(0, 48)
    def _(i):
        time_copy(i).wait_send()

    @pl.when(x < 3)
    def _():
        @pl.loop(0, 64)
        def _(i):
            back(i).wait_send()

    for c in sends + first + sent:
        c.wait_send()


def joined(outs):
    width = -(-len(outs) * HD // 128) * 128
    rows = outs[0].shape[0]
    at = lax.broadcasted_iota(jnp.int32, (rows, 128), 1)
    blank = jnp.zeros((rows, 128), jnp.float32)
    done = []
    for c in range(width // 128):
        piece = blank
        for h, o in enumerate(outs):
            lo = h * HD - c * 128
            if lo >= 128 or lo + HD <= 0:
                continue
            moved = pltpu.roll(o, lo % 128, 1) if lo % 128 else o
            keep = jnp.logical_and(at >= lo, at < lo + HD)
            piece = jnp.where(keep, moved, piece)
        done.append(piece)
    return jnp.concatenate(done, axis=1)


def layer(w_qkv, w_out, rows, boxes, count, valid, link, gate):
    bf, f32 = jnp.bfloat16, jnp.float32
    hbm = pl.BlockSpec(memory_space=pl.ANY)
    vmem = pl.BlockSpec(memory_space=pltpu.VMEM)
    smem = pl.BlockSpec(memory_space=pltpu.SMEM)
    n = TOKENS
    dma = pltpu.SemaphoreType.DMA
    return pl.pallas_call(
        layer_kernel,
        out_shape=jax.ShapeDtypeStruct(rows.shape, bf),
        in_specs=[hbm] * 2 + [vmem] * 2 + [smem] * 3 + [vmem],
        out_specs=vmem,
        scratch_shapes=[
            pltpu.VMEM((4, 16, 72, XC), bf),
            pltpu.VMEM((16, 72, ZW), bf),
            pltpu.VMEM((2, n, D), bf),
            pltpu.VMEM((4, 18, XC + ZW), bf),
            pltpu.VMEM((72, XC + ZW), bf),
            pltpu.VMEM((n, 3 * D), f32),
            pltpu.VMEM((2 * n, 1280), f32),
            pltpu.VMEM((48, 8, 896), bf),
            pltpu.VMEM((64, 8, 896), bf),
            pltpu.VMEM((64, 8, 384), bf),
            pltpu.VMEM((48, 8, 384), bf),
            pltpu.VMEM((16, 640), bf),
            pltpu.VMEM((64, 16, 640), bf),
            pltpu.VMEM((8, n, 128), bf),
            pltpu.VMEM((8, 3 * n, 128), bf),
            pltpu.VMEM((8, 3 * n, 128), bf),
            pltpu.VMEM((4, n, 128), bf),
            pltpu.VMEM((4, n + 1024, 128), bf),
            pltpu.VMEM((4, n + 1024, 128), bf),
            pltpu.VMEM((12, n, 128), f32),
            dma((90,)), dma((4, 3)), dma((4, 16)), dma((16,)), dma((2,)), dma((21,)),
            dma((48,)), dma((64,)), dma((64,)), dma((48,)),
            dma((7,)), dma((8,)), dma((16,)), dma((16,)), dma,
        ],
        compiler_params=pltpu.CompilerParams(
            collective_id=0, has_side_effects=True, vmem_limit_bytes=60 << 20
        ),
        name="layer",
    )(w_qkv, w_out, rows, boxes, count, valid, link, gate)


def per_device(frames_x, box_embed, box_count, frame_valid, cycle_link, w_qkv, w_out, box_gate):
    result = layer(
        w_qkv,
        w_out,
        frames_x.reshape(TOKENS, D),
        box_embed.reshape(16, D),
        box_count,
        frame_valid,
        cycle_link,
        box_gate,
    )
    return result.reshape(frames_x.shape)


def solution(mesh):
    in_specs = (
        P("view", "tm", None, None),
        P("view", "tm", None, None),
        P("view", "tm"),
        P("view", "tm"),
        P("view", None),
        P("tm", None),
        P("tm", None),
        P(),
    )
    out_specs = P("view", "tm", None, None)
    return jax.shard_map(
        per_device, mesh=mesh, in_specs=in_specs, out_specs=out_specs, check_vma=False
    )
```

time: 180 us -> 145 us (0.81)
  the two profiles are of different devices: /device:TPU:12 before, /device:TPU:8 now
where the time goes in v1:
time: 145 us; the launch traced here: 144 us
  Pallas kernels  141 us (97%)
  local copies, waits for them, and re-layouts  2.15 us (1%)
    pallas_call x1, Pallas kernels, layer(): pl.pallas_call(layer_kernel, out_shape=jax.ShapeDtypeStruct(rows.shape, b...  141 us

profile of v1, /device:TPU:8, one launch (start us, length us, event | category | flops | bytes accessed | tf_op | source)
XLA Modules:
  0.0 144.4 jit_solution(7048887354368632294)
XLA Ops:
  1.3 141.0 %layer.1 = bf16[384,1152]{1,0:T(8,128)(2,1)} custom-call(bf16[18,3456]{1,0:T(8,128)(2,1)} %wq.1, bf16[18,1152]{1,0:T(8,128)(2,1)} %wo.1, bf16[384,1152]{1,0:T(8,128)(2,1)} %bitcast.4, bf16[16,1152]{1,0:T(8,128)(2,1)} %bitcast.5, s32[1,1]{1,0:T(1,128)S(6)} %copy.10.cnt_ref, s32[1,1]{1,0:T(1,128)S(6)} %copy.11.val_ref, s32[1,2]{1,0:T(1,128)} %link_ref.1, ...), custom_call_target="tpu_custom_call" | custom-call | tf_op jit(solution)/shard_map/layer/pallas_call | solution.py:462
  142.3 2.1 %copy.12 = bf16[1,1,384,1152]{3,2,1,0:T(8,128)(2,1)} copy(bf16[1,1,384,1152]{3,2,1,0:T(8,128)(2,1)} %bitcast.3) | data formatting | bytes 1769472

commit v2 on v1

--- a/solution.py
+++ b/solution.py
@@ -25,7 +25,7 @@
     wx, wz, xn, m, stage,
     qkv, nbr, tsend, tqkv, tout, timed, kvb, bkv, qc, kc, vc, qb, kb, vb, oh,
     ssem, msem, rxs, rzs, nsem, lsem,
-    ts_send, ts_recv, to_send, to_recv, ba_send, ba_recv, br_send, br_recv, own_sem,
+    ts_send, ts_recv, to_send, to_recv, br_send, br_recv, own_sem,
 ):
     bf, f32 = jnp.bfloat16, jnp.float32
     n = TOKENS
@@ -49,8 +49,7 @@
     def zat(k):
         return lax.rem(z + d * k + 16, 8)
 
-    plane = [tm(yh, z, lax.rem(x + j, 4)) for j in range(1, 4)]
-    plane += [tm(1 - yh, z, lax.rem(x + j, 4)) for j in range(4)]
+    plane = [tm(yh, z, lax.rem(x + j, 4)) for j in range(1, 4)] + [tm(1 - yh, z, x)]
     barrier = pltpu.get_barrier_semaphore()
 
     @pl.loop(0, 64)
@@ -61,7 +60,7 @@
         pl.semaphore_signal(barrier, inc=1, device_id=(v, p), device_id_type=MESH)
     for p in (up, down):
         pl.semaphore_signal(barrier, inc=1, device_id=(p, t), device_id_type=MESH)
-    pl.semaphore_wait(barrier, 75)
+    pl.semaphore_wait(barrier, 72)
 
     sends = []
 
@@ -135,14 +134,17 @@
     def forward(xx, b, to):
         send(wx.at[xx, b], wx.at[xx, b], rxs.at[xx, b], to)
 
-    def spread(b, srcx, srcz, nxt):
+    def spread_x(b, src, nxt):
         for k in nxt:
-            send(srcx, wx.at[x, b], rxs.at[x, b], (v, tm(yh, k, x)))
-            send(srcz, wz.at[b], rzs.at[b], (v, tm(yh, k, x)))
+            send(src, wx.at[x, b], rxs.at[x, b], (v, tm(yh, k, x)))
         for xx in (right, left):
-            send(srcx, wx.at[x, b], rxs.at[x, b], (v, tm(yh, z, xx)))
-        send(srcx, wx.at[x, b], rxs.at[x, b], (partner, t))
-        send(srcz, wz.at[b], rzs.at[b], (partner, t))
+            send(src, wx.at[x, b], rxs.at[x, b], (v, tm(yh, z, xx)))
+        send(src, wx.at[x, b], rxs.at[x, b], (partner, t))
+
+    def spread_z(b, src, nxt):
+        for k in nxt:
+            send(src, wz.at[b], rzs.at[b], (v, tm(yh, k, x)))
+        send(src, wz.at[b], rzs.at[b], (partner, t))
 
     def relay_x(b, sign):
         arrived(wx.at[left, b], rxs.at[left, b])
@@ -158,19 +160,21 @@
         arrived(wx.at[across, b], rxs.at[across, b])
         forward(across, b, (partner, t))
 
-    spread(b0, stage.at[:, pl.ds(0, XC)], stage.at[:, pl.ds(XC, ZW)], (zat(1), zat(-1)))
+    spread_x(b0, stage.at[:, pl.ds(0, XC)], (zat(1), zat(-1)))
+    spread_z(b0, stage.at[:, pl.ds(XC, ZW)], (zat(1), zat(-1)))
     send(x_ref, xn.at[0], nsem.at[0], (up, t))
     send(x_ref, xn.at[1], nsem.at[1], (down, t))
     todo, late = [(b0, -1)], []
     for s in range(1, 5):
-        for sign in (1, -1):
-            if sign < 0 and s == 4:
-                continue
+        signs = (1, -1) if s < 4 else (1,)
+        for sign in signs:
             b = mine + zat(-s * sign)
             arrived(wx.at[x, b], rxs.at[x, b])
+            spread_x(b, wx.at[x, b], (zat(sign),) if s < (4 if sign > 0 else 3) else ())
+        for sign in signs:
+            b = mine + zat(-s * sign)
             arrived(wz.at[b], rzs.at[b])
-            last = s == 4 or (sign < 0 and s == 3)
-            spread(b, wx.at[x, b], wz.at[b], () if last else (zat(sign),))
+            spread_z(b, wz.at[b], (zat(sign),) if s < (4 if sign > 0 else 3) else ())
             todo.append((b, sign))
             b, sign = todo.pop(0)
             relay_x(b, sign)
@@ -210,33 +214,22 @@
     kvb[...] = bv[:, :640].astype(bf)
 
     rows = x_ref[...]
-    qkv[:, 0:XC] = mm(rows, chunk(0, 0, XC))
-
-    own = pltpu.make_async_copy(kvb, bkv.at[t], own_sem)
-    own.start()
-    first = []
-    for k, p in enumerate(plane):
-        c = pltpu.make_async_remote_copy(
-            src_ref=kvb,
-            dst_ref=bkv.at[t],
-            send_sem=ba_send.at[k],
-            recv_sem=ba_recv.at[yh * 4 + x],
-            device_id=(v, p),
-            device_id_type=MESH,
-        )
-        c.start()
-        first.append(c)
-
-    for i in range(1, 4):
-        qkv[:, i * XC : (i + 1) * XC] = mm(rows, chunk(i, 0, XC))
-    qkv[:, QX : QX + ZQ] = mm(rows, tail(0, ZQ))
-
-    tq = [qkv[:, c * 128 : c * 128 + 896] for c in (4, 13)]
-    tq.append(jnp.concatenate([qkv[:, 2816:3456], qkv[:, 0:256]], axis=1))
+    spots = (
+        (512, chunk(0, 512, 768)),
+        (768, chunk(1, 0, 128)),
+        (1664, chunk(2, 128, 512)),
+        (2816, chunk(3, 512, 768)),
+        (3072, tail(0, 128)),
+    )
+    for lo, w in spots:
+        qkv[:, lo : lo + w.shape[1]] = mm(rows, w)
     lane = lax.broadcasted_iota(jnp.int32, (n, 896), 1)
-    packed = pltpu.roll(tq[0], 896 - 64, 1)
-    packed = jnp.where(lane < 288, packed, pltpu.roll(tq[1], 288 - 64, 1))
-    packed = jnp.where(lane < 576, packed, pltpu.roll(tq[2], 576 - 64, 1))
+    blank = jnp.zeros((n, 512), f32)
+    parts = [
+        pltpu.roll(jnp.concatenate([qkv[:, lo : lo + 384], blank], axis=1), shift, 1)
+        for lo, shift in ((512, 896 - 64), (1664, 288 - 64), (2816, 576 - 64))
+    ]
+    packed = jnp.where(lane < 288, parts[0], jnp.where(lane < 576, parts[1], parts[2]))
     tsend[...] = packed.astype(bf).reshape(48, 8, 896)
 
     def time_copy(i):
@@ -255,47 +248,73 @@
         def _(i):
             time_copy(i).start()
 
-    own.wait()
-    for yy in range(2):
-        for j in range(4):
-            if yy or j:
-                half, xx = lax.rem(yh + yy, 2), lax.rem(x + j, 4)
-                arrived(bkv.at[tm(half, z, xx)], ba_recv.at[half * 4 + xx])
-
-    def group(yy, zz):
-        return bkv.at[pl.ds(tm(yy, zz, 0), 4)]
-
-    def ring(yy, zz, to, k):
-        return pltpu.make_async_remote_copy(
-            src_ref=group(yy, zz),
-            dst_ref=group(yy, zz),
-            send_sem=br_send.at[k],
-            recv_sem=br_recv.at[yy * 8 + zz],
-            device_id=(v, tm(yh, to, x)),
+    sent = []
+
+    def pass_on(slot, to, src=None):
+        c = pltpu.make_async_remote_copy(
+            src_ref=bkv.at[slot] if src is None else src,
+            dst_ref=bkv.at[slot],
+            send_sem=br_send.at[len(sent)],
+            recv_sem=br_recv.at[slot],
+            device_id=(v, to),
             device_id_type=MESH,
         )
-
-    sent = []
-
-    def start(c):
         c.start()
         sent.append(c)
 
-    for yy in range(2):
-        for sign in (1, -1):
-            start(ring(yy, z, zat(sign), len(sent)))
+    def landed(slot):
+        arrived(bkv.at[slot], br_recv.at[slot])
+
+    own = pltpu.make_async_copy(kvb, bkv.at[t], own_sem)
+    own.start()
+    pass_on(t, tm(1 - yh, z, x), kvb)
+    for to in (tm(yh, zat(1), x), tm(yh, zat(-1), x), tm(yh, z, right), tm(yh, z, left)):
+        pass_on(t, to, kvb)
+    send_time(0, 16)
+
+    spots = (
+        (0, chunk(0, 0, 512)),
+        (896, chunk(1, 128, 768)),
+        (1536, chunk(2, 0, 128)),
+        (2048, chunk(2, 512, 768)),
+        (2304, chunk(3, 0, 512)),
+        (3200, tail(128, 384)),
+    )
+    for lo, w in spots:
+        qkv[:, lo : lo + w.shape[1]] = mm(rows, w)
+
+    own.wait()
+    landed(tm(1 - yh, z, x))
+    for to in (tm(yh, zat(1), x), tm(yh, zat(-1), x), tm(yh, z, right), tm(yh, z, left)):
+        pass_on(tm(1 - yh, z, x), to)
+
+    boxes_x, boxes_late = [(z, -1)], []
 
     def relay(s):
-        for sign in (1, -1):
-            if sign < 0 and s == 4:
-                continue
+        for sign in (1, -1) if s < 4 else (1,):
             zz = zat(-s * sign)
-            for yy in range(2):
-                arrived(group(yy, zz), br_recv.at[yy * 8 + zz])
+            for half in (yh, 1 - yh):
+                slot = tm(half, zz, x)
+                landed(slot)
                 if s < (4 if sign > 0 else 3):
-                    start(ring(yy, zz, zat(sign), len(sent)))
-
-    send_time(0, 24)
+                    pass_on(slot, tm(yh, zat(sign), x))
+                pass_on(slot, tm(yh, z, right))
+                pass_on(slot, tm(yh, z, left))
+            boxes_x.append((zz, sign))
+
+    def relay_boxes(keep):
+        while len(boxes_x) > keep:
+            zz, sign = boxes_x.pop(0)
+            for half in (yh, 1 - yh):
+                landed(tm(half, zz, left))
+                if sign > 0:
+                    pass_on(tm(half, zz, left), tm(yh, z, right))
+                landed(tm(half, zz, right))
+                if sign < 0:
+                    pass_on(tm(half, zz, right), tm(yh, z, left))
+            boxes_late.append(zz)
+
+    send_time(16, 32)
 
     arrived(xn.at[0], nsem.at[0])
     arrived(xn.at[1], nsem.at[1])
@@ -303,6 +322,10 @@
     nbr[:, 0:384] = mm(near, chunk(1, 384, 768))
     nbr[:, 384:640] = mm(near, chunk(2, 0, 256))
     nbr[:, 640:1280] = mm(near, chunk(3, 0, 640))
+
+    relay(1)
+    relay_boxes(2)
+    send_time(32, 48)
 
     def tile(a, off, fill):
         piece = pltpu.roll(a, (a.shape[1] - off) % a.shape[1], 1)[:, :128] if off else a[:, :128]
@@ -346,10 +369,11 @@
                 oh[out0 + h, r : r + 128] = o * (1.0 / o[:, HD : HD + 1])
 
     for s in range(1, 5):
-        relay(s)
-        if s == 1:
-            send_time(24, 48)
+        if s > 1:
+            relay(s)
+            relay_boxes(2)
         heads(2 * (s - 1), 2, qc, kc, vc, 0)
+    relay_boxes(0)
 
     @pl.loop(0, 64)
     def _(i):
@@ -388,6 +412,9 @@
             outs.append(o * (1.0 / o[:, HD : HD + 1]))
         tout[...] = joined(outs).astype(bf).reshape(64, 8, 384)
 
+    for zz in boxes_late:
+        for half in (yh, 1 - yh):
+            landed(tm(half, zz, across))
     for r in range(0, 1024, 256):
         a = bkv[r // 16 : r // 16 + 16].reshape(256, 640).astype(f32)
         fill = a[:, 576:577]
@@ -429,7 +456,7 @@
         def _(i):
             back(i).wait_send()
 
-    for c in sends + first + sent:
+    for c in sends + sent:
         c.wait_send()
 
 
@@ -487,7 +514,7 @@
             pltpu.VMEM((12, n, 128), f32),
             dma((90,)), dma((4, 3)), dma((4, 16)), dma((16,)), dma((2,)), dma((21,)),
             dma((48,)), dma((64,)), dma((64,)), dma((48,)),
-            dma((7,)), dma((8,)), dma((16,)), dma((16,)), dma,
+            dma((64,)), dma((64,)), dma,
         ],
         compiler_params=pltpu.CompilerParams(
             collective_id=0, has_side_effects=True, vmem_limit_bytes=60 << 20

time: 145 us -> 133 us (0.917)
  the two profiles are of different devices: /device:TPU:8 before, /device:TPU:1 now
where the time goes in v2:
time: 133 us; the launch traced here: 132 us
  Pallas kernels  129 us (97%)
  local copies, waits for them, and re-layouts  2.15 us (2%)
    pallas_call x1, Pallas kernels, layer(): pl.pallas_call(layer_kernel, out_shape=jax.ShapeDtypeStruct(rows.shape, b...  129 us

profile of v2, /device:TPU:1, one launch (start us, length us, event | category | flops | bytes accessed | tf_op | source)
XLA Modules:
  0.0 132.3 jit_solution(15597855128632187671)
XLA Ops:
  1.3 128.9 %layer.1 = bf16[384,1152]{1,0:T(8,128)(2,1)} custom-call(bf16[18,3456]{1,0:T(8,128)(2,1)} %wq.1, bf16[18,1152]{1,0:T(8,128)(2,1)} %wo.1, bf16[384,1152]{1,0:T(8,128)(2,1)} %bitcast.4, bf16[16,1152]{1,0:T(8,128)(2,1)} %bitcast.5, s32[1,1]{1,0:T(1,128)S(6)} %copy.10.cnt_ref, s32[1,1]{1,0:T(1,128)S(6)} %copy.11.val_ref, s32[1,2]{1,0:T(1,128)} %link_ref.1, ...), custom_call_target="tpu_custom_call" | custom-call | tf_op jit(solution)/shard_map/layer/pallas_call | solution.py:489
  130.2 2.1 %copy.12 = bf16[1,1,384,1152]{3,2,1,0:T(8,128)(2,1)} copy(bf16[1,1,384,1152]{3,2,1,0:T(8,128)(2,1)} %bitcast.3) | data formatting | bytes 1769472

commit v3 on v2

--- a/solution.py
+++ b/solution.py
@@ -40,7 +40,6 @@
     partner = v + 1 - 2 * core
     v4 = lax.rem(v + 4, 8)
     owner = (t // 4) * 3 + x
-    base = (t * 3) // 4
     right, left, across = [lax.rem(x + j, 4) for j in (1, 3, 2)]
 
     def tm(yy, zz, xx):
@@ -82,10 +81,10 @@
     @pl.when(core == yh)
     def _():
         out = []
-        for half, view in ((yh, v), (1 - yh, v4)):
-            for j in (2, 1, 3, 0):
-                xx = lax.rem(x + j, 4)
-                cols = pl.ds(pl.multiple_of(xx * XC, 128), XC)
+        for j in (2, 1, 3, 0):
+            xx = lax.rem(x + j, 4)
+            cols = pl.ds(pl.multiple_of(xx * XC, 128), XC)
+            for half, view in ((1 - yh, v4), (yh, v)):
                 for k, (src, lo, width) in enumerate(
                     (
                         (wq.at[:, cols], 0, XC),
@@ -232,14 +231,20 @@
     packed = jnp.where(lane < 288, parts[0], jnp.where(lane < 576, parts[1], parts[2]))
     tsend[...] = packed.astype(bf).reshape(48, 8, 896)
 
+    def zfar(j):
+        k = 7 - j
+        h = (k + 1) // 2
+        return lax.rem(z + h * (2 * lax.rem(k, 2) - 1) + 8, 8)
+
     def time_copy(i):
-        o = lax.rem(i + base, 48)
+        half, zz, xx = lax.rem(yh + i, 2), zfar(i // 6), lax.rem(x + i // 2, 3)
+        o = (half * 8 + zz) * 3 + xx
         return pltpu.make_async_remote_copy(
             src_ref=tsend.at[o],
             dst_ref=tqkv.at[t],
             send_sem=ts_send.at[i],
             recv_sem=ts_recv.at[t],
-            device_id=(v4, (o // 3) * 4 + lax.rem(o, 3)),
+            device_id=(v4, tm(half, zz, xx)),
             device_id_type=MESH,
         )
 
@@ -384,7 +389,7 @@
             pltpu.make_async_copy(ref, ref, ts_recv.at[i]).wait()
 
     def back(i):
-        f = lax.rem(i + t, 64)
+        f = tm(lax.rem(yh + i, 2), zfar(i // 8), lax.rem(x + i // 2, 4))
         return pltpu.make_async_remote_copy(
             src_ref=tout.at[f],
             dst_ref=timed.at[owner],

time: 133 us -> 133 us (level)
  no operation moved by 1% of the time
where the time goes in v3:
time: 133 us
  Pallas kernels  130 us (98%)
  local copies, waits for them, and re-layouts  2.15 us (2%)
    pallas_call x1, Pallas kernels, layer(): pl.pallas_call(layer_kernel, out_shape=jax.ShapeDtypeStruct(rows.shape, b...  130 us

profile of v3, /device:TPU:1, one launch (start us, length us, event | category | flops | bytes accessed | tf_op | source)
XLA Modules:
  0.0 133.1 jit_solution(4243404668254370756)
XLA Ops:
  1.3 129.6 %layer.1 = bf16[384,1152]{1,0:T(8,128)(2,1)} custom-call(bf16[18,3456]{1,0:T(8,128)(2,1)} %wq.1, bf16[18,1152]{1,0:T(8,128)(2,1)} %wo.1, bf16[384,1152]{1,0:T(8,128)(2,1)} %bitcast.4, bf16[16,1152]{1,0:T(8,128)(2,1)} %bitcast.5, s32[1,1]{1,0:T(1,128)S(6)} %copy.10.cnt_ref, s32[1,1]{1,0:T(1,128)S(6)} %copy.11.val_ref, s32[1,2]{1,0:T(1,128)} %link_ref.1, ...), custom_call_target="tpu_custom_call" | custom-call | tf_op jit(solution)/shard_map/layer/pallas_call | solution.py:494
  130.9 2.1 %copy.12 = bf16[1,1,384,1152]{3,2,1,0:T(8,128)(2,1)} copy(bf16[1,1,384,1152]{3,2,1,0:T(8,128)(2,1)} %bitcast.3) | data formatting | bytes 1769472

commit v4 on v3

--- a/solution.py
+++ b/solution.py
@@ -417,6 +417,12 @@
             outs.append(o * (1.0 / o[:, HD : HD + 1]))
         tout[...] = joined(outs).astype(bf).reshape(64, 8, 384)
 
+    @pl.when(x < 3)
+    def _():
+        @pl.loop(0, 64)
+        def _(i):
+            back(i).start()
+
     for zz in boxes_late:
         for half in (yh, 1 - yh):
             landed(tm(half, zz, across))
@@ -426,12 +432,6 @@
         for h in range(BOX_HEADS):
             kb[h, n + r : n + r + 256] = tile(a, HD * h, fill)
             vb[h, n + r : n + r + 256] = tile(a, 288 + HD * h, 1.0)
-
-    @pl.when(x < 3)
-    def _():
-        @pl.loop(0, 64)
-        def _(i):
-            back(i).start()
 
     heads(0, BOX_HEADS, qb, kb, vb, CROSS_HEADS)
 

time: 133 us -> 133 us (level)
  no operation moved by 1% of the time
where the time goes in v4:
time: 133 us
  Pallas kernels  129 us (97%)
  local copies, waits for them, and re-layouts  2.15 us (2%)
    pallas_call x1, Pallas kernels, layer(): pl.pallas_call(layer_kernel, out_shape=jax.ShapeDtypeStruct(rows.shape, b...  129 us

profile of v4, /device:TPU:1, one launch (start us, length us, event | category | flops | bytes accessed | tf_op | source)
XLA Modules:
  0.0 132.5 jit_solution(9684098278236130777)
XLA Ops:
  1.3 129.1 %layer.1 = bf16[384,1152]{1,0:T(8,128)(2,1)} custom-call(bf16[18,3456]{1,0:T(8,128)(2,1)} %wq.1, bf16[18,1152]{1,0:T(8,128)(2,1)} %wo.1, bf16[384,1152]{1,0:T(8,128)(2,1)} %bitcast.4, bf16[16,1152]{1,0:T(8,128)(2,1)} %bitcast.5, s32[1,1]{1,0:T(1,128)S(6)} %copy.10.cnt_ref, s32[1,1]{1,0:T(1,128)S(6)} %copy.11.val_ref, s32[1,2]{1,0:T(1,128)} %link_ref.1, ...), custom_call_target="tpu_custom_call" | custom-call | tf_op jit(solution)/shard_map/layer/pallas_call | solution.py:494
  130.4 2.1 %copy.12 = bf16[1,1,384,1152]{3,2,1,0:T(8,128)(2,1)} copy(bf16[1,1,384,1152]{3,2,1,0:T(8,128)(2,1)} %bitcast.3) | data formatting | bytes 1769472
